TPU v7x, 32 devices: a whole 2x2x4 slice. The times are simulated.
32 devices in a mesh: event: 8 (over z, core), mesh: 4 (over y, x).
Axes of the slice: x: 2, y: 2, z: 4, core: 2. Of those that a mesh axis runs over, the one named last changes fastest.
Arguments:
- forward_start: float32 [8, 3, 125, 512], P('event', None, None, 'mesh'), may hold values from -6 to 6
- adjoint_start: float32 [8, 3, 125, 512], P('event', None, None, 'mesh'), may hold values from -6 to 6
- stiffness: float32 [125, 125], replicated
- projection: float32 [125, 64], replicated, may hold values from -0.5 to 0.5
- material: float32 [8, 512], P('event', 'mesh'), may hold values from 0.5 to 2
- neighbours: int32 [8, 6, 512], P('event', None, 'mesh'), may hold values from 0 to 511, as said below
- destinations: int32 [8, 512], P('event', 'mesh'), may hold values from 0 to 127
- counts: int32 [8, 4], P('event', 'mesh'), may hold values from 32 to 128, as said below
- smoothing: float32 [4, 128], P(None, ('event', 'mesh')), may hold values from 0.02 to 0.12
Outputs:
- forward_final: float32 [8, 3, 125, 512], P('event', None, None, 'mesh')
- tiles: float32 [64, 128], P(None, ('event', 'mesh'))
Inputs may be any that keep to these rules, and one draw needn't show every extreme that they name: `counts`: in every event one partition holds exactly 128 live elements and another exactly 32; live elements fill a partition's first slots. `neighbours`: A neighbour slot lies in the element's own partition, or in the previous or next partition of the same event (wrapping around), and then among that partition's first 32 slots.
All inputs are finite; a program needn't handle non-finite values.
Results may differ from a plain program's by a relative error of at most 0.0003.
Values sent between devices are 32-bit elements; how exact they have to be, the bound alone decides.
A program may use at most 64 MiB of HBM per device.

v0:
```python
import math

import jax
import jax.numpy as jnp
from jax import lax
from jax.sharding import PartitionSpec as P

STEPS = 2


time_square = 0.4
penalty = 0.5
partner_face = (1, 0, 3, 2, 5, 4)


def padded_2(x, sides, width, wrap):
    for axis, dim in sides:
        count, length = (lax.axis_size(axis), x.shape[dim])
        up = [(i, (i + 1) % count) for i in range(count if wrap else count - 1)]
        down = [(j, i) for i, j in up]
        last = lax.slice_in_dim(x, length - width, length, axis=dim)
        first = lax.slice_in_dim(x, 0, width, axis=dim)
        before = lax.ppermute(last, axis, up)
        after = lax.ppermute(first, axis, down)
        x = jnp.concatenate([before, x, after], axis=dim)
    return x


def element_faces(field):
    elements = field.shape[-1]
    cube = field.reshape(3, 5, 5, 5, elements)
    sheets = [
        cube[:, 0],
        cube[:, 4],
        cube[:, :, 0],
        cube[:, :, 4],
        cube[:, :, :, 0],
        cube[:, :, :, 4],
    ]
    return jnp.stack(sheets).reshape(6, 3, 25, elements)


def lift_faces(jumps):
    elements = jumps.shape[-1]
    sheets = jumps.reshape(6, 3, 5, 5, elements)
    keep = (0, 0)
    lifted = jnp.pad(sheets[0][:, None], (keep, (0, 4), keep, keep, keep))
    lifted = lifted + jnp.pad(sheets[1][:, None], (keep, (4, 0), keep, keep, keep))
    lifted = lifted + jnp.pad(sheets[2][:, :, None], (keep, keep, (0, 4), keep, keep))
    lifted = lifted + jnp.pad(sheets[3][:, :, None], (keep, keep, (4, 0), keep, keep))
    lifted = lifted + jnp.pad(sheets[4][:, :, :, None], (keep, keep, keep, (0, 4), keep))
    lifted = lifted + jnp.pad(sheets[5][:, :, :, None], (keep, keep, keep, (4, 0), keep))
    return lifted.reshape(3, 125, elements)


def node_laplace(values, coefs):
    width = values.shape[-1]
    cube = values.reshape(4, 4, 4, width)
    padded = jnp.pad(cube, ((1, 1), (1, 1), (1, 1), (0, 0)))
    first_dir = padded[2:, 1:-1, 1:-1] + padded[:-2, 1:-1, 1:-1] - 2.0 * cube
    second_dir = padded[1:-1, 2:, 1:-1] + padded[1:-1, :-2, 1:-1] - 2.0 * cube
    third_dir = padded[1:-1, 1:-1, 2:] + padded[1:-1, 1:-1, :-2] - 2.0 * cube
    summed = coefs[0] * first_dir + coefs[1] * second_dir + coefs[2] * third_dir
    return summed.reshape(64, width)


def smooth_columns(values, coefs):
    middle = values[:, 1:-1]
    chain = values[:, :-2] + values[:, 2:] - 2.0 * middle
    return middle + coefs[0] * chain + node_laplace(middle, coefs[1:])


def per_device(
    forward_start,
    adjoint_start,
    stiffness,
    projection,
    material,
    neighbours,
    destinations,
    counts,
    smoothing,
):
    elements = forward_start.shape[-1]
    boundary = elements // 4
    tile_width = smoothing.shape[1]
    mesh_size = lax.axis_size("mesh")
    event_size = lax.axis_size("event")
    my_partition = lax.axis_index("mesh")
    slots = jnp.arange(elements, dtype=jnp.int32)
    live = (slots < counts[0, 0]).astype(jnp.float32)
    fields = jnp.stack([forward_start[0], adjoint_start[0]]) * live
    previous = fields
    target = neighbours[0] // elements
    local_slot = neighbours[0] % elements
    relative = (target - my_partition + mesh_size) % mesh_size
    pool_index = jnp.where(
        relative == 0,
        local_slot,
        jnp.where(relative == 1, elements + 2 * boundary + local_slot, elements + local_slot),
    )
    material_row = material[0]
    kernel = jnp.zeros((stiffness.shape[0], elements), jnp.float32)
    for step_index in range(STEPS):
        strain = jnp.einsum("nm,fcme->fcne", stiffness, fields, precision=lax.Precision.HIGHEST)
        kernel = kernel + jnp.sum(fields[0] * strain[1], axis=0)
        faces = jax.vmap(element_faces)(fields)
        rim_slab = padded_2(fields[..., :boundary], (("mesh", 3),), boundary, True)
        rim_faces = jax.vmap(element_faces)(rim_slab)
        pool = jnp.concatenate([faces, rim_faces], axis=4)
        across = jnp.stack(
            [jnp.take(pool[:, partner_face[face]], pool_index[face], axis=3) for face in range(6)],
            axis=1,
        )
        force = -material_row * strain + penalty * jax.vmap(lift_faces)(across - faces)
        following = live * (2.0 * fields - previous + time_square * force)
        previous, fields = (fields, following)
    scale = math.sqrt(tile_width / elements) / STEPS
    blocks = jnp.dot(projection.T, kernel, precision=lax.Precision.HIGHEST) * scale
    total_tiles = tile_width * event_size * mesh_size
    destination_row = destinations[0]
    dense = (
        jnp.zeros((projection.shape[1], total_tiles), jnp.float32)
        .at[:, destination_row]
        .add(blocks)
    )
    tiles = lax.psum_scatter(dense, ("event", "mesh"), scatter_dimension=1, tiled=True)
    for pass_index in range(2):
        padded = padded_2(tiles, ((("event", "mesh"), 1),), 1, False)
        tiles = smooth_columns(padded, smoothing)
    return (fields[0][None], tiles)


def solution(mesh):
    in_specs = (
        P("event", None, None, "mesh"),
        P("event", None, None, "mesh"),
        P(),
        P(),
        P("event", "mesh"),
        P("event", None, "mesh"),
        P("event", "mesh"),
        P("event", "mesh"),
        P(None, ("event", "mesh")),
    )
    out_specs = (P("event", None, None, "mesh"), P(None, ("event", "mesh")))
    return jax.shard_map(
        per_device, mesh=mesh, in_specs=in_specs, out_specs=out_specs, check_vma=False
    )
```

profile of v0, /device:TPU:0, one launch (start us, length us, event | category | flops | bytes accessed | tf_op | source)
XLA Modules:
  0.0 131.2 jit_solution(15426055095323881984)
XLA Ops:
  1.3 1.1 copy.150
  2.7 3.0 %collective-permute-start = (f32[2,3,125,32]{2,3,1,0:T(8,128)S(1)}, f32[2,3,125,32]{2,3,1,0:T(8,128)S(1)}, u32[]{:S(2)}, u32[]{:S(2)}) collective-permute-start(f32[2,3,125,32]{2,3,1,0:T(8,128)S(1)} %slice.389), channel_id=1, source_target_pairs={{0,1},{1,2},{2,3},{3,0},{4,5},{5,6},{6,7},{7,4},{8,9},{9,10},{10,1... | collective-permute-start | bytes 288008 | tf_op jit(solution)/shard_map/ppermute | solution.py:23
  5.7 1.0 collective-permute-start.1
  6.8 0.4 maximum_multiply_fusion.1
  7.3 0.7 copy-done.12
  8.2 0.6 copy-done.16
  8.8 0.5 fusion.76
  9.5 0.7 collective-permute-done
  10.1 1.7 %collective-permute-done.1 = f32[2,3,125,32]{2,3,1,0:T(8,128)S(1)} collective-permute-done((f32[2,3,125,32]{2,3,1,0:T(8,128)S(1)}, f32[2,3,125,32]{2,3,1,0:T(8,128)S(1)}, u32[]{:S(2)}, u32[]{:S(2)}) %collective-permute-start.1) | collective-permute-done | bytes 96032 | tf_op jit(solution)/shard_map/ppermute | solution.py:24
  12.3 0.4 pad_maximum_fusion.3
  12.7 0.9 copy.218
  13.6 1.9 %gather_fusion = f32[128,2,3,25]{3,1,2,0:T(2,128)} fusion(f32[2,3,25,224]{2,0,3,1:T(2,128)S(1)} %bitcast.327, s32[1024]{0:T(1024)S(1)} %pad_clamp_fusion.5), kind=kCustom, calls=%fused_computation.clone | custom fusion | bytes 154112 | tf_op jit(solution)/shard_map/jit(_take)/gather | solution.py:112
  15.5 1.2 select_bitcast_fusion.11
  17.0 0.9 copy.219
  17.8 1.1 gather_fusion.1
  19.0 0.2 select_bitcast_fusion.10
  19.5 0.9 copy.220
  20.3 1.1 gather_fusion.2
  21.9 0.9 copy.221
  22.8 1.1 gather_fusion.3
  24.4 0.9 copy.222
  25.3 1.1 gather_fusion.4
  26.9 0.9 copy.223
  27.8 1.1 gather_fusion.5
  30.4 1.3 fusion.1
  32.0 1.6 %collective-permute-start.2 = (f32[2,3,125,32]{2,3,1,0:T(8,128)S(1)}, f32[2,3,125,32]{2,3,1,0:T(8,128)S(1)}, u32[]{:S(2)}, u32[]{:S(2)}) collective-permute-start(f32[2,3,125,32]{2,3,1,0:T(8,128)S(1)} %slice.418), channel_id=1, source_target_pairs={{0,1},{1,2},{2,3},{3,0},{4,5},{5,6},{6,7},{7,4},{8,9},{9,10},{10,1... | collective-permute-start | bytes 288008 | tf_op jit(solution)/shard_map/ppermute | solution.py:23
  33.6 1.4 %collective-permute-start.3 = (f32[2,3,125,32]{2,3,1,0:T(8,128)S(1)}, f32[2,3,125,32]{2,3,1,0:T(8,128)S(1)}, u32[]{:S(2)}, u32[]{:S(2)}) collective-permute-start(f32[2,3,125,32]{2,3,1,0:T(8,128)S(1)} %slice.418), channel_id=1, source_target_pairs={{1,0},{2,1},{3,2},{0,3},{5,4},{6,5},{7,6},{4,7},{9,8},{10,9},{11,1... | collective-permute-start | bytes 288008 | tf_op jit(solution)/shard_map/ppermute | solution.py:24
  35.0 0.5 convolution_bitcast_fusion
  35.6 1.9 %collective-permute-done.2 = f32[2,3,125,32]{2,3,1,0:T(8,128)S(1)} collective-permute-done((f32[2,3,125,32]{2,3,1,0:T(8,128)S(1)}, f32[2,3,125,32]{2,3,1,0:T(8,128)S(1)}, u32[]{:S(2)}, u32[]{:S(2)}) %collective-permute-start.2) | collective-permute-done | bytes 96032 | tf_op jit(solution)/shard_map/ppermute | solution.py:23
  37.6 0.7 collective-permute-done.3
  38.7 0.4 pad_maximum_fusion.2
  39.1 0.9 copy.240
  40.0 1.8 %gather_fusion.10 = f32[128,2,3,25]{3,1,2,0:T(2,128)} fusion(f32[2,3,25,224]{2,0,3,1:T(2,128)S(1)} %bitcast.321, s32[1024]{0:T(1024)S(1)} %pad_clamp_fusion.1), kind=kCustom, calls=%fused_computation.10.clone | custom fusion | bytes 154112 | tf_op jit(solution)/shard_map/jit(_take)/gather | solution.py:112
  41.8 0.9 copy.241
  42.7 1.9 %gather_fusion.11 = f32[128,2,3,25]{3,1,2,0:T(2,128)} fusion(f32[2,3,25,224]{2,0,3,1:T(2,128)S(1)} %bitcast.322, s32[1024]{0:T(1024)S(1)} %pad_clamp_fusion), kind=kCustom, calls=%fused_computation.11.clone | custom fusion | bytes 154112 | tf_op jit(solution)/shard_map/jit(_take)/gather | solution.py:112
  44.6 1.7 %select_bitcast_fusion = (f32[2,3,25,128]{2,0,1,3:T(2,128)S(1)}, f32[2,3,25,128]{2,0,1,3:T(2,128)S(1)}) fusion(f32[128,2,3,25]{3,1,2,0:T(2,128)} %gather_fusion.11, pred[128]{0:T(512)(128)(4,1)S(1)} %copy-done.9, f32[128,2,3,25]{3,1,2,0:T(2,128)} %gather_fusion.10, pred[128]{0:T(512)(128)(4,1)S(1)} %copy-done.11), kind=kLoop, calls=%fused_computation.42 | loop fusion | flops 38400 | bytes 307456 | tf_op jit(solution)/shard_map/jit(_take)/select_n | solution.py:112
  46.3 0.9 copy.199
  47.2 0.9 copy.238
  48.0 1.9 %gather_fusion.8 = f32[128,2,3,25]{3,1,2,0:T(2,128)} fusion(f32[2,3,25,224]{2,0,3,1:T(2,128)S(1)} %bitcast.323, s32[1024]{0:T(1024)S(1)} %pad_clamp_fusion.3), kind=kCustom, calls=%fused_computation.8.clone | custom fusion | bytes 154112 | tf_op jit(solution)/shard_map/jit(_take)/gather | solution.py:112
  49.9 0.9 copy.239
  50.8 1.8 %gather_fusion.9 = f32[128,2,3,25]{3,1,2,0:T(2,128)} fusion(f32[2,3,25,224]{2,0,3,1:T(2,128)S(1)} %bitcast.324, s32[1024]{0:T(1024)S(1)} %pad_clamp_fusion.2), kind=kCustom, calls=%fused_computation.9.clone | custom fusion | bytes 154112 | tf_op jit(solution)/shard_map/jit(_take)/gather | solution.py:112
  52.6 1.7 %select_bitcast_fusion.2 = (f32[2,3,25,128]{2,0,1,3:T(2,128)S(1)}, f32[2,3,25,128]{2,0,1,3:T(2,128)S(1)}) fusion(f32[128,2,3,25]{3,1,2,0:T(2,128)} %gather_fusion.9, pred[128]{0:T(512)(128)(4,1)S(1)} %get-tuple-element.52, f32[128,2,3,25]{3,1,2,0:T(2,128)} %gather_fusion.8, pred[128]{0:T(512)(128)(4,1)S(1)} %get-tuple-element.54), kind=kLoop, calls=%fused_computation.44 | loop fusion | flops 38400 | bytes 307456 | tf_op jit(solution)/shard_map/jit(_take)/select_n | solution.py:112
  54.3 0.9 copy.195
  55.2 0.9 copy.236
  56.1 1.9 %gather_fusion.6 = f32[128,2,3,25]{3,1,2,0:T(2,128)} fusion(f32[2,3,25,224]{2,0,3,1:T(2,128)S(1)} %bitcast.325, s32[1024]{0:T(1024)S(1)} %pad_clamp_fusion.5), kind=kCustom, calls=%fused_computation.6.clone | custom fusion | bytes 154112 | tf_op jit(solution)/shard_map/jit(_take)/gather | solution.py:112
  57.9 0.9 copy.237
  58.8 1.8 %gather_fusion.7 = f32[128,2,3,25]{3,1,2,0:T(2,128)} fusion(f32[2,3,25,224]{2,0,3,1:T(2,128)S(1)} %bitcast.326, s32[1024]{0:T(1024)S(1)} %pad_clamp_fusion.4), kind=kCustom, calls=%fused_computation.7.clone | custom fusion | bytes 154112 | tf_op jit(solution)/shard_map/jit(_take)/gather | solution.py:112
  60.6 1.7 %select_bitcast_fusion.4 = (f32[2,3,25,128]{2,0,1,3:T(2,128)S(1)}, f32[2,3,25,128]{2,0,1,3:T(2,128)S(1)}) fusion(f32[128,2,3,25]{3,1,2,0:T(2,128)} %gather_fusion.7, pred[128]{0:T(512)(128)(4,1)S(1)} %get-tuple-element.56, f32[128,2,3,25]{3,1,2,0:T(2,128)} %gather_fusion.6, pred[128]{0:T(512)(128)(4,1)S(1)} %get-tuple-element.58), kind=kLoop, calls=%fused_computation.46 | loop fusion | flops 38400 | bytes 307456 | tf_op jit(solution)/shard_map/jit(_take)/select_n | solution.py:112
  62.6 0.6 constant_dynamic-update-slice_fusion.11
  64.0 0.5 copy-done.4
  64.5 0.9 copy-done.6
  65.5 0.9 copy-done.5
  67.3 0.7 copy-done.1
  68.1 0.6 copy-done.7
  69.1 1.2 scatter_custom_fusion
  70.3 40.6 %all-reduce.14 = f32[64,128]{0,1:T(8,128)S(1)} all-reduce(f32[64,128]{0,1:T(8,128)S(1)} %scatter_custom_fusion), channel_id=2, replica_groups=mesh['event'=8,'mesh'=4] {'event','mesh'}, use_global_device_ids=true, to_apply=%region_3.5.clone | all-reduce | flops 8192 | bytes 65536
  111.0 4.2 %collective-permute-start.4 = (f32[64,1]{0,1:T(1,128)S(1)}, f32[64,1]{0,1:T(1,128)S(1)}, u32[]{:S(2)}, u32[]{:S(2)}) collective-permute-start(f32[64,1]{0,1:T(1,128)S(1)} %get-tuple-element.70), channel_id=1, source_target_pairs={{0,1},{1,2},{2,3},{3,4},{4,5},{5,6},{6,7},{7,8},{8,9},{9,10},{10,1... | collective-permute-start | bytes 776 | tf_op jit(solution)/shard_map/ppermute | solution.py:23
  115.1 1.3 collective-permute-start.5
  116.6 0.8 copy.208
  117.5 3.1 %collective-permute-done.5 = f32[64,1]{0,1:T(1,128)S(1)} collective-permute-done((f32[64,1]{0,1:T(1,128)S(1)}, f32[64,1]{0,1:T(1,128)S(1)}, u32[]{:S(2)}, u32[]{:S(2)}) %collective-permute-start.5) | collective-permute-done | bytes 288 | tf_op jit(solution)/shard_map/ppermute | solution.py:24
  120.8 4.3 %collective-permute-start.6 = (f32[64,1]{0,1:T(1,128)S(1)}, f32[64,1]{0,1:T(1,128)S(1)}, u32[]{:S(2)}, u32[]{:S(2)}) collective-permute-start(f32[64,1]{0,1:T(1,128)S(1)} %get-tuple-element.62), channel_id=1, source_target_pairs={{0,1},{1,2},{2,3},{3,4},{4,5},{5,6},{6,7},{7,8},{8,9},{9,10},{10,1... | collective-permute-start | bytes 776 | tf_op jit(solution)/shard_map/ppermute | solution.py:23
  125.1 1.3 collective-permute-start.7
  126.6 3.9 %collective-permute-done.7 = f32[64,1]{0,1:T(1,128)S(1)} collective-permute-done((f32[64,1]{0,1:T(1,128)S(1)}, f32[64,1]{0,1:T(1,128)S(1)}, u32[]{:S(2)}, u32[]{:S(2)}) %collective-permute-start.7) | collective-permute-done | bytes 288 | tf_op jit(solution)/shard_map/ppermute | solution.py:24
  130.5 0.7 add_add_fusion
  (128 shorter events, 8.3 us)
Async XLA Ops:
  0.6 29.8 %copy-start = (f32[125,125]{1,0:T(8,128)S(1)}, f32[125,125]{1,0:T(8,128)}, u32[]{:S(2)}) copy-start(f32[125,125]{1,0:T(8,128)} %param.13) | copy-start | bytes 187504
  1.3 1.1 copy-start.2
  2.7 4.1 %copy-start.3 = (f32[1,3,125,128]{3,0,2,1:T(1,128)S(1)}, f32[1,3,125,128]{3,0,2,1:T(1,128)}, u32[]{:S(2)}) copy-start(f32[1,3,125,128]{3,0,2,1:T(1,128)} %param.11) | copy-start | bytes 576004
  2.7 7.4 %collective-permute-start = (f32[2,3,125,32]{2,3,1,0:T(8,128)S(1)}, f32[2,3,125,32]{2,3,1,0:T(8,128)S(1)}, u32[]{:S(2)}, u32[]{:S(2)}) collective-permute-start(f32[2,3,125,32]{2,3,1,0:T(8,128)S(1)} %slice.389), channel_id=1, source_target_pairs={{0,1},{1,2},{2,3},{3,0},{4,5},{5,6},{6,7},{7,4},{8,9},{9,10},{10,1... | collective-permute-start | bytes 288008 | tf_op jit(solution)/shard_map/ppermute | solution.py:23
  5.7 6.1 %collective-permute-start.1 = (f32[2,3,125,32]{2,3,1,0:T(8,128)S(1)}, f32[2,3,125,32]{2,3,1,0:T(8,128)S(1)}, u32[]{:S(2)}, u32[]{:S(2)}) collective-permute-start(f32[2,3,125,32]{2,3,1,0:T(8,128)S(1)} %slice.389), channel_id=1, source_target_pairs={{1,0},{2,1},{3,2},{0,3},{5,4},{6,5},{7,6},{4,7},{9,8},{10,9},{11,1... | collective-permute-start | bytes 288008 | tf_op jit(solution)/shard_map/ppermute | solution.py:24
  7.3 0.7 copy-start.12
  8.0 0.8 copy-start.17
  8.0 18.4 %copy-start.10 = (pred[128]{0:T(512)(128)(4,1)}, pred[128]{0:T(512)(128)(4,1)S(1)}, u32[]{:S(2)}) copy-start(pred[128]{0:T(512)(128)(4,1)S(1)} %get-tuple-element.50) | copy-start | bytes 388
  8.1 20.8 %copy-start.8 = (pred[128]{0:T(512)(128)(4,1)}, pred[128]{0:T(512)(128)(4,1)S(1)}, u32[]{:S(2)}) copy-start(pred[128]{0:T(512)(128)(4,1)S(1)} %get-tuple-element.11) | copy-start | bytes 388
  8.1 0.7 copy-start.16
  8.8 0.7 copy-start.15
  8.8 21.6 %copy-start.13 = (f32[128]{0:T(128)}, f32[128]{0:T(128)S(1)}, u32[]{:S(2)}) copy-start(f32[128]{0:T(128)S(1)} %negate_bitcast_fusion) | copy-start | bytes 1540
  32.0 5.6 %collective-permute-start.2 = (f32[2,3,125,32]{2,3,1,0:T(8,128)S(1)}, f32[2,3,125,32]{2,3,1,0:T(8,128)S(1)}, u32[]{:S(2)}, u32[]{:S(2)}) collective-permute-start(f32[2,3,125,32]{2,3,1,0:T(8,128)S(1)} %slice.418), channel_id=1, source_target_pairs={{0,1},{1,2},{2,3},{3,0},{4,5},{5,6},{6,7},{7,4},{8,9},{9,10},{10,1... | collective-permute-start | bytes 288008 | tf_op jit(solution)/shard_map/ppermute | solution.py:23
  33.6 4.6 %collective-permute-start.3 = (f32[2,3,125,32]{2,3,1,0:T(8,128)S(1)}, f32[2,3,125,32]{2,3,1,0:T(8,128)S(1)}, u32[]{:S(2)}, u32[]{:S(2)}) collective-permute-start(f32[2,3,125,32]{2,3,1,0:T(8,128)S(1)} %slice.418), channel_id=1, source_target_pairs={{1,0},{2,1},{3,2},{0,3},{5,4},{6,5},{7,6},{4,7},{9,8},{10,9},{11,1... | collective-permute-start | bytes 288008 | tf_op jit(solution)/shard_map/ppermute | solution.py:24
  42.7 1.9 %copy-start.9 = (pred[128]{0:T(512)(128)(4,1)S(1)}, pred[128]{0:T(512)(128)(4,1)}, u32[]{:S(2)}) copy-start(pred[128]{0:T(512)(128)(4,1)} %copy-done.8) | copy-start | bytes 388
  42.7 1.9 %copy-start.11 = (pred[128]{0:T(512)(128)(4,1)S(1)}, pred[128]{0:T(512)(128)(4,1)}, u32[]{:S(2)}) copy-start(pred[128]{0:T(512)(128)(4,1)} %copy-done.10) | copy-start | bytes 388
  63.5 1.0 copy-start.4
  64.5 0.9 copy-start.6
  65.4 0.9 copy-start.5
  67.0 1.0 copy-start.1
  67.3 0.7 copy-start.14
  68.0 0.8 copy-start.7
  111.0 6.5 %collective-permute-start.4 = (f32[64,1]{0,1:T(1,128)S(1)}, f32[64,1]{0,1:T(1,128)S(1)}, u32[]{:S(2)}, u32[]{:S(2)}) collective-permute-start(f32[64,1]{0,1:T(1,128)S(1)} %get-tuple-element.70), channel_id=1, source_target_pairs={{0,1},{1,2},{2,3},{3,4},{4,5},{5,6},{6,7},{7,8},{8,9},{9,10},{10,1... | collective-permute-start | bytes 776 | tf_op jit(solution)/shard_map/ppermute | solution.py:23
  115.1 5.5 %collective-permute-start.5 = (f32[64,1]{0,1:T(1,128)S(1)}, f32[64,1]{0,1:T(1,128)S(1)}, u32[]{:S(2)}, u32[]{:S(2)}) collective-permute-start(f32[64,1]{0,1:T(1,128)S(1)} %get-tuple-element.71), channel_id=1, source_target_pairs={{1,0},{2,1},{3,2},{4,3},{5,4},{6,5},{7,6},{8,7},{9,8},{10,9},{11,1... | collective-permute-start | bytes 776 | tf_op jit(solution)/shard_map/ppermute | solution.py:24
  120.8 5.8 %collective-permute-start.6 = (f32[64,1]{0,1:T(1,128)S(1)}, f32[64,1]{0,1:T(1,128)S(1)}, u32[]{:S(2)}, u32[]{:S(2)}) collective-permute-start(f32[64,1]{0,1:T(1,128)S(1)} %get-tuple-element.62), channel_id=1, source_target_pairs={{0,1},{1,2},{2,3},{3,4},{4,5},{5,6},{6,7},{7,8},{8,9},{9,10},{10,1... | collective-permute-start | bytes 776 | tf_op jit(solution)/shard_map/ppermute | solution.py:23
  125.1 5.5 %collective-permute-start.7 = (f32[64,1]{0,1:T(1,128)S(1)}, f32[64,1]{0,1:T(1,128)S(1)}, u32[]{:S(2)}, u32[]{:S(2)}) collective-permute-start(f32[64,1]{0,1:T(1,128)S(1)} %get-tuple-element.63), channel_id=1, source_target_pairs={{1,0},{2,1},{3,2},{4,3},{5,4},{6,5},{7,6},{8,7},{9,8},{10,9},{11,1... | collective-permute-start | bytes 776 | tf_op jit(solution)/shard_map/ppermute | solution.py:24
where the time goes:
time: 132 us; the launch traced here: 131 us
  local copies, waits for them, and re-layouts  43.6 us (33%)
  blocking collectives  40.6 us (31%)
  starting transfers between devices  18 us (14%)
  other arithmetic  12.8 us (10%)
  waiting for transfers between devices  12 us (9%)
  between operations  2.22 us (2%)
  matrix products  2.03 us (2%)
    unnamed x1, blocking collectives  40.6 us
    unnamed x85, local copies, waits for them, and re-layouts  18.8 us
    gather x12, local copies, waits for them, and re-layouts, per_device(): jnp.take(pool[:, partner_face[face]], pool_index[face], axis=3)  18.6 us
    ppermute x4, starting transfers between devices, padded_2(): before = lax.ppermute(last, axis, up)  13.1 us
    ppermute x4, waiting for transfers between devices, padded_2(): after = lax.ppermute(first, axis, down)  9.43 us
    select_n x9, other arithmetic, per_device(): jnp.take(pool[:, partner_face[face]], pool_index[face], axis=3)  7.67 us
    ppermute x4, starting transfers between devices, padded_2(): after = lax.ppermute(first, axis, down)  4.96 us
    select_n x12, local copies, waits for them, and re-layouts, per_device(): jnp.take(pool[:, partner_face[face]], pool_index[face], axis=3)  4.12 us
  transfers between devices with their start and end apart: 8, of which 6 were waited for; matrix products, arithmetic and copies ran while one was open for 2% of the time, Pallas kernels for 0%

commit v1 on v0

v1 whole, which is shorter than its diff:
```python
import functools
import math

import jax
import jax.numpy as jnp
from jax import lax
from jax.experimental import pallas as pl
from jax.experimental.pallas import tpu as pltpu
from jax.sharding import PartitionSpec as P

STEPS = 2
time_square = 0.4
penalty = 0.5

PAD = 8
ROWS = 128
NODES = 125
SHIFT = (100, -100, 20, -20, 4, -4)
MESH = pl.DeviceIdType.MESH
f32 = jnp.float32
bf16 = jnp.bfloat16


def on_face(face, node):
    i, j, k = node // 25, (node // 5) % 5, node % 5
    return (i == 0, i == 4, j == 0, j == 4, k == 0, k == 4)[face]


TILE_FACES = [
    [f for f in range(6) if any(on_face(f, n) for n in range(8 * t, min(8 * t + 8, NODES)))]
    for t in range(ROWS // 8)
]


def split(x):
    high = x.astype(bf16)
    return high, (x - high.astype(f32)).astype(bf16)


def mm(a, b, dims=((1,), (0,))):
    return lax.dot_general(a, b, (dims, ((), ())), preferred_element_type=f32)


def pick(x, index):
    return jnp.take_along_axis(x, index, axis=1, mode="promise_in_bounds")


def kernel(
    m_size, e_size,
    fwd_in, adj_in, stiff_in, proj_in, mat_in, nb_in, dest_in, count_in, smooth_in,
    fwd_out, tiles_out,
    F, N, K, S, W, IDX, LIVE, send, rim, rim2, coef, coef_in, msg, part, got, mine, got2,
    rim_s, rim_r, rim2_s, rim2_r, coef_s, coef_r, a_s, a_r, b_s, b_r,
):
    me = lax.axis_index("mesh")
    ev = lax.axis_index("event")
    total = m_size * e_size
    lin = ev * m_size + me
    after = lax.rem(me + 1, m_size)
    before = lax.rem(me + m_size - 1, m_size)
    nxt = lax.rem(lin + 1, total)
    prv = lax.rem(lin + total - 1, total)
    lin_id = lambda d: (lax.div(d, m_size), lax.rem(d, m_size))

    barrier = pltpu.get_barrier_semaphore()
    partners = [(ev, lax.rem(me + j, m_size)) for j in range(1, m_size)]
    partners += [(lax.rem(ev + j, e_size), me) for j in range(1, e_size)]
    partners += [lin_id(nxt), lin_id(prv)]
    for device in partners:
        pl.semaphore_signal(barrier, inc=1, device_id=device, device_id_type=MESH)

    lane = lax.broadcasted_iota(jnp.int32, (1, 128), 1)
    live = jnp.where(lane < count_in[0:1, 0:1], 1.0, 0.0).astype(f32)
    LIVE[...] = jnp.broadcast_to(live, (8, 128))
    zero8 = jnp.zeros((PAD, 128), f32)
    for fc in range(6):
        source = fwd_in if fc < 3 else adj_in
        F[fc, 0:PAD, :] = zero8
        F[fc, 128:136, :] = zero8
        F[fc, 136:144, :] = zero8
        F[fc, PAD : PAD + NODES, :] = source[0, fc % 3] * live

    def pack(base):
        wide = [F[base + c, PAD : PAD + ROWS, :] for c in range(3)]
        head = jnp.where(
            lane < 32,
            wide[0][:96],
            jnp.where(lane < 64, pltpu.roll(wide[1][:96], 32, 1), pltpu.roll(wide[2][:96], 64, 1)),
        )
        tail = pltpu.roll(jnp.concatenate([w[96:] for w in wide], axis=0), 96, 1)
        return jnp.where(lane < 96, head, tail)

    send[0] = pack(0)
    send[1] = pack(3)
    coef[...] = jnp.zeros((8, 128), f32)
    coef[0:4, 0:4] = smooth_in[...]

    pl.semaphore_wait(barrier, len(partners))

    def remote(src, dst, s, r, device):
        copy = pltpu.make_async_remote_copy(
            src_ref=src, dst_ref=dst, send_sem=s, recv_sem=r, device_id=device, device_id_type=MESH
        )
        copy.start()
        return copy

    rim_copies = [
        [
            remote(send.at[f], rim.at[f, 0, pl.ds(PAD, 96)], rim_s.at[f, 0], rim_r.at[f, 0], (ev, after)),
            remote(send.at[f], rim.at[f, 1, pl.ds(PAD, 96)], rim_s.at[f, 1], rim_r.at[f, 1], (ev, before)),
        ]
        for f in range(2)
    ]
    coef_copies = [
        remote(coef, coef_in.at[0], coef_s.at[0], coef_r.at[0], lin_id(nxt)),
        remote(coef, coef_in.at[1], coef_s.at[1], coef_r.at[1], lin_id(prv)),
    ]

    node = lax.broadcasted_iota(jnp.int32, (ROWS, 128), 0).astype(f32)
    i = jnp.floor((node + 0.5) / 25.0)
    rest = node - 25.0 * i
    j = jnp.floor((rest + 0.5) / 5.0)
    k = rest - 5.0 * j
    count = jnp.zeros((ROWS, 128), f32)
    for f, test in enumerate((i == 0.0, i == 4.0, j == 0.0, j == 4.0, k == 0.0, k == 4.0)):
        mask = jnp.where(test & (node < NODES - 0.5), 1.0, 0.0).astype(f32)
        W[f] = mask
        count = count + mask
    W[6] = count
    nb = nb_in[0]
    target = lax.shift_right_logical(nb, 7)
    slot = nb & 127
    relative = lax.rem(target - me + m_size, m_size)
    for f in range(6):
        IDX[f] = jnp.broadcast_to(slot[f : f + 1], (8, 128))
        IDX[6 + f] = jnp.broadcast_to(relative[f : f + 1], (8, 128))
    S[...] = jnp.zeros((ROWS, ROWS), f32)
    S[0:NODES, 0:NODES] = stiff_in[...]
    s_hi, s_lo = split(S[...])
    material = mat_in[...]

    def strain(base):
        wide = jnp.concatenate([F[base + c, PAD : PAD + ROWS, :] for c in range(3)], axis=1)
        hi, lo = split(wide)
        both = mm(s_hi, hi) + (mm(s_hi, lo) + mm(s_lo, hi))
        return [both[:, 128 * c : 128 * (c + 1)] for c in range(3)]

    def own_pass(base):
        def body(c, carry):
            for t in range(ROWS // 8):
                acc = jnp.zeros((8, 128), f32)
                for f in TILE_FACES[t]:
                    x = F[base + c, 8 * t + PAD + SHIFT[f] : 8 * t + 2 * PAD + SHIFT[f], :]
                    g = pick(x, IDX[f])
                    acc = acc + jnp.where(IDX[6 + f] == 0, g, 0.0) * W[f, 8 * t : 8 * t + 8, :]
                v = F[base + c, 8 * t + PAD : 8 * t + 2 * PAD, :]
                acc = acc - W[6, 8 * t : 8 * t + 8, :] * v
                N[base + c, 8 * t : 8 * t + 8, :] = (
                    N[base + c, 8 * t : 8 * t + 8, :] + (time_square * penalty) * acc
                )
            return carry

        lax.fori_loop(0, 3, body, 0)

    def unpack(ref):
        pieces = [
            pltpu.roll(ref[PAD + 32 * c : PAD + 32 * c + 32, :], 32 * (c + 1), 1) for c in range(3)
        ]
        ref[PAD + 96 : PAD + 128, :] = jnp.where(
            lane < 32, pieces[0], jnp.where(lane < 64, pieces[1], pieces[2])
        )
        ref[0:PAD, :] = zero8
        ref[PAD + 128 : PAD + 136, :] = zero8

    def rim_pass(base, ref, store):
        def body(c, carry):
            live8 = LIVE[...]
            for t in range(ROWS // 8):
                acc = jnp.zeros((8, 128), f32)
                for f in TILE_FACES[t]:
                    low = 8 * t + PAD + SHIFT[f]
                    at = (IDX[f] & 31) + 32 * c
                    r = IDX[6 + f]
                    g = jnp.where(
                        r == 1, pick(ref[1, low : low + 8, :], at), pick(ref[0, low : low + 8, :], at)
                    )
                    acc = acc + jnp.where(r == 0, 0.0, g) * W[f, 8 * t : 8 * t + 8, :]
                old = N[base + c, 8 * t : 8 * t + 8, :]
                store(c, t, live8 * (old + (time_square * penalty) * acc))
            return carry

        lax.fori_loop(0, 3, body, 0)

    st_f = strain(0)
    st_a = strain(3)
    energy = jnp.zeros((ROWS, 128), f32)
    for c in range(3):
        vf = F[c, PAD : PAD + ROWS, :]
        energy = energy + vf * st_a[c]
        N[c] = vf - time_square * material * st_f[c]
        N[3 + c] = F[3 + c, PAD : PAD + ROWS, :] - time_square * material * st_a[c]
    K[...] = energy
    own_pass(0)
    own_pass(3)

    def keep(base):
        def store(c, t, value):
            at = pl.ds(8 * t + PAD, 8)
            if base == 0:
                N[c, 8 * t : 8 * t + 8, :] = 2.0 * value - F[c, at, :]
            F[base + c, at, :] = value

        return store

    for f in range(2):
        for side in range(2):
            rim_copies[f][side].wait_recv()
            unpack(rim.at[f, side])
        rim_pass(3 * f, rim.at[f], keep(3 * f))
        if f == 0:
            send[2] = pack(0)
            rim2_copies = [
                remote(send.at[2], rim2.at[0, pl.ds(PAD, 96)], rim2_s.at[0], rim2_r.at[0], (ev, after)),
                remote(send.at[2], rim2.at[1, pl.ds(PAD, 96)], rim2_s.at[1], rim2_r.at[1], (ev, before)),
            ]

    st_a = strain(3)
    energy = K[...]
    for c in range(3):
        energy = energy + F[c, PAD : PAD + ROWS, :] * st_a[c]
    elements = fwd_in.shape[-1]
    width = smooth_in.shape[1]
    scale = math.sqrt(width / elements) / STEPS
    twin = jnp.concatenate([proj_in[...], proj_in[...]], axis=1)
    K[...] = energy
    blocks = lax.dot_general(
        twin, K[0:NODES, :], (((0,), (0,)), ((), ())),
        preferred_element_type=f32, precision=lax.Precision.HIGHEST,
    ) * scale
    b_hi, b_lo = split(blocks)
    rows = total * width
    row = lax.broadcasted_iota(jnp.int32, (rows, 128), 0)
    owner = lax.div(row, width)
    tile = width * (lax.rem(owner, e_size) * m_size + lax.div(owner, e_size)) + lax.rem(row, width)
    dest = dest_in[...]
    nt = ((1,), (1,))

    def spread(offset):
        hot = jnp.where(tile + offset == dest, 1.0, 0.0).astype(f32).astype(bf16)
        return mm(hot, b_hi, nt) + mm(hot, b_lo, nt)

    packed = jnp.where(lane < 64, spread(-2), spread(2))
    msg[...] = packed.reshape(m_size, e_size, width, 128)
    a_copies = [
        remote(msg.at[lax.rem(me + o, m_size)], got.at[o - 1], a_s.at[o - 1], a_r.at[o - 1],
               (ev, lax.rem(me + o, m_size)))
        for o in range(1, m_size)
    ]

    st_f = strain(0)
    for c in range(3):
        N[c] = N[c] - time_square * material * st_f[c]
    own_pass(0)

    for copy in a_copies:
        copy.wait_recv()
    mine_sum = msg[me]
    for o in range(m_size - 1):
        mine_sum = mine_sum + got[o]
    part[...] = mine_sum
    b_copies = [
        remote(part.at[lax.rem(ev + o, e_size)], got2.at[o - 1], b_s.at[o - 1], b_r.at[o - 1],
               (lax.rem(ev + o, e_size), me))
        for o in range(1, e_size)
    ]

    for side in range(2):
        rim2_copies[side].wait_recv()
        unpack(rim2.at[side])

    def final(c, t, value):
        size = min(8, NODES - 8 * t)
        fwd_out[0, c, 8 * t : 8 * t + size, :] = value[:size]

    rim_pass(0, rim2, final)

    for copy in coef_copies:
        copy.wait_recv()
    own_coef = pltpu.roll(coef[...], 2, 1)
    left = jnp.where(lin > 0, coef_in[0], 0.0)
    right = jnp.where(lin < total - 1, coef_in[1], 0.0)
    left = jnp.where(lane < 2, pltpu.roll(left, 126, 1), 0.0)
    right = pltpu.roll(right, 6, 1)
    coefs = own_coef + left + right

    for copy in b_copies:
        copy.wait_recv()
    summed = part[ev]
    for o in range(e_size - 1):
        summed = summed + got2[o]
    mine[...] = jnp.zeros((128, 128), f32)
    mine[0:width, :] = summed
    turned = mine[...].T
    x = jnp.where(lane < 4, turned[0:64], pltpu.roll(turned[64:128], 4, 1))
    x = jnp.where(lane < 8, x, 0.0)
    r64 = lax.broadcasted_iota(jnp.int32, (64, 128), 0)
    for _ in range(2):
        chain = pltpu.roll(x, 1, 1) + pltpu.roll(x, 127, 1) - 2.0 * x
        new = x + coefs[0:1] * chain
        for d, stride in ((1, 16), (2, 4), (3, 1)):
            digit = lax.shift_right_logical(r64, {16: 4, 4: 2, 1: 0}[stride]) & 3
            up = jnp.where(digit == 0, 0.0, pltpu.roll(x, stride, 0))
            down = jnp.where(digit == 3, 0.0, pltpu.roll(x, 64 - stride, 0))
            new = new + coefs[d : d + 1] * (up + down - 2.0 * x)
        x = jnp.where(lane < 8, new, 0.0)
    tiles_out[...] = pltpu.roll(x, 126, 1)[:, 0:width]

    for copy in rim_copies[0] + rim_copies[1] + rim2_copies + coef_copies + a_copies + b_copies:
        copy.wait_send()


def solution(mesh):
    m_size, e_size = mesh.shape["mesh"], mesh.shape["event"]
    in_specs = (
        P("event", None, None, "mesh"),
        P("event", None, None, "mesh"),
        P(),
        P(),
        P("event", "mesh"),
        P("event", None, "mesh"),
        P("event", "mesh"),
        P("event", "mesh"),
        P(None, ("event", "mesh")),
    )
    out_specs = (P("event", None, None, "mesh"), P(None, ("event", "mesh")))

    def per_device(*args):
        fwd, smoothing = args[0], args[-1]
        width = smoothing.shape[1]
        dma = pltpu.SemaphoreType.DMA
        vmem = pl.BlockSpec(memory_space=pltpu.VMEM)
        return pl.pallas_call(
            functools.partial(kernel, m_size, e_size),
            out_shape=(
                jax.ShapeDtypeStruct(fwd.shape, f32),
                jax.ShapeDtypeStruct((64, width), f32),
            ),
            in_specs=[vmem] * len(args),
            out_specs=(vmem, vmem),
            scratch_shapes=[
                pltpu.VMEM((6, 144, 128), f32),
                pltpu.VMEM((6, ROWS, 128), f32),
                pltpu.VMEM((ROWS, 128), f32),
                pltpu.VMEM((ROWS, ROWS), f32),
                pltpu.VMEM((7, ROWS, 128), f32),
                pltpu.VMEM((12, 8, 128), jnp.int32),
                pltpu.VMEM((8, 128), f32),
                pltpu.VMEM((3, 96, 128), f32),
                pltpu.VMEM((2, 2, 144, 128), f32),
                pltpu.VMEM((2, 144, 128), f32),
                pltpu.VMEM((8, 128), f32),
                pltpu.VMEM((2, 8, 128), f32),
                pltpu.VMEM((m_size, e_size, width, 128), f32),
                pltpu.VMEM((e_size, width, 128), f32),
                pltpu.VMEM((m_size - 1, e_size, width, 128), f32),
                pltpu.VMEM((128, 128), f32),
                pltpu.VMEM((e_size - 1, width, 128), f32),
                dma((2, 2)), dma((2, 2)), dma((2,)), dma((2,)), dma((2,)), dma((2,)),
                dma((m_size - 1,)), dma((m_size - 1,)), dma((e_size - 1,)), dma((e_size - 1,)),
            ],
            compiler_params=pltpu.CompilerParams(collective_id=0, has_side_effects=True),
        )(*args)

    return jax.shard_map(
        per_device, mesh=mesh, in_specs=in_specs, out_specs=out_specs, check_vma=False
    )
```

time: 132 us -> 33 us (0.25)
  blocking collectives: 40.6 us -> 0 us
  local copies, waits for them, and re-layouts: 43.6 us -> 7.58 us
  Pallas kernels: 0 us -> 23.9 us
  starting transfers between devices: 18 us -> 0 us
  other arithmetic: 12.8 us -> 0 us
  waiting for transfers between devices: 12 us -> 0 us
  matrix products: 2.03 us -> 0 us
    unnamed x1 -> x0, blocking collectives: 40.6 us -> none
    pallas_call x0 -> x1, Pallas kernels: none -> 23.9 us  [per_device(): pl.pallas_call(functools.partial(kernel, m_size, e_size), out_shape=(jax....]
    gather x12 -> x0, local copies, waits for them, and re-layouts: 18.6 us -> none  [per_device(): jnp.take(pool[:, partner_face[face]], pool_index[face], axis=3)]
    ppermute x8 -> x0, starting transfers between devices: 18 us -> none  [the longest x4 13.1 us: padded_2(): before = lax.ppermute(last, axis, up)]
    unnamed x85 -> x8, local copies, waits for them, and re-layouts: 18.8 us -> 5.12 us
    ppermute x8 -> x0, waiting for transfers between devices: 12 us -> none  [the longest x4 9.43 us: padded_2(): after = lax.ppermute(first, axis, down)]
    select_n x11 -> x0, other arithmetic: 8.24 us -> none  [the longest x9 7.67 us: per_device(): jnp.take(pool[:, partner_face[face]], pool_index[face], axis=3)]
    select_n x12 -> x0, local copies, waits for them, and re-layouts: 4.12 us -> none  [per_device(): jnp.take(pool[:, partner_face[face]], pool_index[face], axis=3)]
  transfers between devices with their start and end apart: 8 -> 0, of which waited for: 6 -> 0; matrix products, arithmetic and copies ran while one was open for 2% -> 0% of each run, Pallas kernels for 0% -> 0%
where the time goes in v1:
time: 33 us; the launch traced here: 32.8 us
  Pallas kernels  23.9 us (72%)
  local copies, waits for them, and re-layouts  7.58 us (23%)
  between operations  1.3 us (4%)
    pallas_call x1, Pallas kernels, per_device(): pl.pallas_call(functools.partial(kernel, m_size, e_size), out_shape=(jax....  23.9 us
    unnamed x8, local copies, waits for them, and re-layouts  5.12 us
    pallas_call x2, local copies, waits for them, and re-layouts, per_device(): pl.pallas_call(functools.partial(kernel, m_size, e_size), out_shape=(jax....  2.46 us

profile of v1, /device:TPU:0, one launch (start us, length us, event | category | flops | bytes accessed | tf_op | source)
XLA Modules:
  0.0 32.8 jit_solution(6458935956892672025)
XLA Ops:
  1.3 1.3 %copy.14.nb_in = s32[1,6,128]{2,1,0:T(8,128)} copy(s32[1,6,128]{2,0,1:T(1,128)} %param.14) | data formatting | bytes 6144 | tf_op args[5]
  2.6 1.5 %copy.13.proj_in = f32[125,64]{1,0:T(8,128)} copy(f32[125,64]{0,1:T(8,128)} %param.12) | data formatting | bytes 64000 | tf_op args[3]
  4.0 0.0 copy-start
  4.1 1.6 %copy.11.fwd_in = f32[1,3,125,128]{3,2,1,0:T(8,128)} copy(f32[1,3,125,128]{3,0,2,1:T(1,128)} %param.9) | data formatting | bytes 384000 | tf_op args[0]
  5.7 0.0 copy-done
  5.7 0.7 %copy.12.adj_in = f32[1,3,125,128]{3,2,1,0:T(8,128)} copy(f32[1,3,125,128]{3,0,2,1:T(1,128)S(1)} %copy-done) | data formatting | bytes 384000 | tf_op args[1]
  6.4 23.9 %shard_map.104 = (f32[1,3,125,128]{3,2,1,0:T(8,128)}, f32[64,4]{1,0:T(8,128)}) custom-call(f32[1,3,125,128]{3,2,1,0:T(8,128)} %copy.11.fwd_in, f32[1,3,125,128]{3,2,1,0:T(8,128)} %copy.12.adj_in, f32[125,125]{1,0:T(8,128)} %stiff_in.1, f32[125,64]{1,0:T(8,128)} %copy.13.proj_in, f32[1,128]{1,0:T(1,128)} %mat_in.1, s32[1,6,128]{2,1,0:T(8,128)} %copy.14.nb_in, ...), custom_call_target="tpu_custom_call" | custom-call | tf_op jit(solution)/shard_map/pallas_call | solution.py:342
  30.3 0.0 copy-start.1
  30.3 1.8 %copy.15 = f32[1,3,125,128]{3,0,2,1:T(1,128)} copy(f32[1,3,125,128]{3,2,1,0:T(8,128)} %get-tuple-element.2) | data formatting | bytes 384000 | tf_op jit(solution)/shard_map/pallas_call | solution.py:342
  32.1 0.0 copy-done.1
  32.1 0.7 %copy.16 = f32[64,4]{0,1:T(4,128)} copy(f32[64,4]{1,0:T(8,128)S(1)} %copy-done.1) | data formatting | bytes 2048 | tf_op jit(solution)/shard_map/pallas_call | solution.py:342
Async XLA Ops:
  4.0 1.6 %copy-start = (f32[1,3,125,128]{3,0,2,1:T(1,128)S(1)}, f32[1,3,125,128]{3,0,2,1:T(1,128)}, u32[]{:S(2)}) copy-start(f32[1,3,125,128]{3,0,2,1:T(1,128)} %param.10) | copy-start | bytes 576004
  30.3 1.8 %copy-start.1 = (f32[64,4]{1,0:T(8,128)S(1)}, f32[64,4]{1,0:T(8,128)}, u32[]{:S(2)}) copy-start(f32[64,4]{1,0:T(8,128)} %get-tuple-element.3) | copy-start | bytes 3076

commit v2 on v1

--- a/solution.py
+++ b/solution.py
@@ -50,7 +50,7 @@
     fwd_in, adj_in, stiff_in, proj_in, mat_in, nb_in, dest_in, count_in, smooth_in,
     fwd_out, tiles_out,
     F, N, K, S, W, IDX, LIVE, send, rim, rim2, coef, coef_in, msg, part, got, mine, got2,
-    rim_s, rim_r, rim2_s, rim2_r, coef_s, coef_r, a_s, a_r, b_s, b_r,
+    in_s, out_s, rim_s, rim_r, rim2_s, rim2_r, coef_s, coef_r, a_s, a_r, b_s, b_r,
 ):
     me = lax.axis_index("mesh")
     ev = lax.axis_index("event")
@@ -62,6 +62,15 @@
     prv = lax.rem(lin + total - 1, total)
     lin_id = lambda d: (lax.div(d, m_size), lax.rem(d, m_size))
 
+    loads = []
+    for fc in range(6):
+        source = fwd_in if fc < 3 else adj_in
+        load = pltpu.make_async_copy(
+            source.at[pl.ds(NODES * (fc % 3), NODES), 0], F.at[fc, pl.ds(PAD, NODES)], in_s.at[fc]
+        )
+        load.start()
+        loads.append(load)
+
     barrier = pltpu.get_barrier_semaphore()
     partners = [(ev, lax.rem(me + j, m_size)) for j in range(1, m_size)]
     partners += [(lax.rem(ev + j, e_size), me) for j in range(1, e_size)]
@@ -74,11 +83,8 @@
     LIVE[...] = jnp.broadcast_to(live, (8, 128))
     zero8 = jnp.zeros((PAD, 128), f32)
     for fc in range(6):
-        source = fwd_in if fc < 3 else adj_in
         F[fc, 0:PAD, :] = zero8
-        F[fc, 128:136, :] = zero8
-        F[fc, 136:144, :] = zero8
-        F[fc, PAD : PAD + NODES, :] = source[0, fc % 3] * live
+        F[fc, PAD + NODES : 144, :] = jnp.zeros((144 - PAD - NODES, 128), f32)
 
     def pack(base):
         wide = [F[base + c, PAD : PAD + ROWS, :] for c in range(3)]
@@ -90,8 +96,10 @@
         tail = pltpu.roll(jnp.concatenate([w[96:] for w in wide], axis=0), 96, 1)
         return jnp.where(lane < 96, head, tail)
 
-    send[0] = pack(0)
-    send[1] = pack(3)
+    for f in range(2):
+        for load in loads[3 * f : 3 * f + 3]:
+            load.wait()
+        send[f] = pack(3 * f)
     coef[...] = jnp.zeros((8, 128), f32)
     coef[0:4, 0:4] = smooth_in[...]
 
@@ -116,6 +124,9 @@
         remote(coef, coef_in.at[1], coef_s.at[1], coef_r.at[1], lin_id(prv)),
     ]
 
+    for fc in range(6):
+        F[fc, PAD : PAD + NODES, :] = F[fc, PAD : PAD + NODES, :] * live
+
     node = lax.broadcasted_iota(jnp.int32, (ROWS, 128), 0).astype(f32)
     i = jnp.floor((node + 0.5) / 25.0)
     rest = node - 25.0 * i
@@ -127,7 +138,7 @@
         W[f] = mask
         count = count + mask
     W[6] = count
-    nb = nb_in[0]
+    nb = nb_in[:, 0, :]
     target = lax.shift_right_logical(nb, 7)
     slot = nb & 127
     relative = lax.rem(target - me + m_size, m_size)
@@ -231,12 +242,11 @@
     elements = fwd_in.shape[-1]
     width = smooth_in.shape[1]
     scale = math.sqrt(width / elements) / STEPS
-    twin = jnp.concatenate([proj_in[...], proj_in[...]], axis=1)
+    twin = jnp.concatenate([proj_in[...], proj_in[...]], axis=0)
     K[...] = energy
-    blocks = lax.dot_general(
-        twin, K[0:NODES, :], (((0,), (0,)), ((), ())),
-        preferred_element_type=f32, precision=lax.Precision.HIGHEST,
-    ) * scale
+    t_hi, t_lo = split(twin)
+    k_hi, k_lo = split(K[0:NODES, :])
+    blocks = (mm(t_hi, k_hi) + (mm(t_hi, k_lo) + mm(t_lo, k_hi))) * scale
     b_hi, b_lo = split(blocks)
     rows = total * width
     row = lax.broadcasted_iota(jnp.int32, (rows, 128), 0)
@@ -279,10 +289,16 @@
         unpack(rim2.at[side])
 
     def final(c, t, value):
-        size = min(8, NODES - 8 * t)
-        fwd_out[0, c, 8 * t : 8 * t + size, :] = value[:size]
+        N[c, 8 * t : 8 * t + 8, :] = value
 
     rim_pass(0, rim2, final)
+    stores = []
+    for c in range(3):
+        store = pltpu.make_async_copy(
+            N.at[c, pl.ds(0, NODES)], fwd_out.at[pl.ds(NODES * c, NODES), 0], out_s.at[c]
+        )
+        store.start()
+        stores.append(store)
 
     for copy in coef_copies:
         copy.wait_recv()
@@ -291,30 +307,31 @@
     right = jnp.where(lin < total - 1, coef_in[1], 0.0)
     left = jnp.where(lane < 2, pltpu.roll(left, 126, 1), 0.0)
     right = pltpu.roll(right, 6, 1)
-    coefs = own_coef + left + right
+    mine[...] = jnp.zeros((128, 128), f32)
+    mine[0:8, :] = own_coef + left + right
+    coefs = mine[...].T[0:8]
+
+    def smooth(x):
+        chain = pltpu.roll(x, 1, 0) + pltpu.roll(x, 7, 0) - 2.0 * x
+        new = x + coefs[:, 0:1] * chain
+        for d, shift in ((1, 4), (2, 2), (3, 0)):
+            digit = lax.shift_right_logical(lane, shift) & 3
+            up = jnp.where(digit == 0, 0.0, pltpu.roll(x, 1 << shift, 1))
+            down = jnp.where(digit == 3, 0.0, pltpu.roll(x, 128 - (1 << shift), 1))
+            new = new + coefs[:, d : d + 1] * (up + down - 2.0 * x)
+        return jnp.where(lane < 64, new, 0.0)
 
     for copy in b_copies:
         copy.wait_recv()
     summed = part[ev]
     for o in range(e_size - 1):
         summed = summed + got2[o]
-    mine[...] = jnp.zeros((128, 128), f32)
-    mine[0:width, :] = summed
-    turned = mine[...].T
-    x = jnp.where(lane < 4, turned[0:64], pltpu.roll(turned[64:128], 4, 1))
-    x = jnp.where(lane < 8, x, 0.0)
-    r64 = lax.broadcasted_iota(jnp.int32, (64, 128), 0)
-    for _ in range(2):
-        chain = pltpu.roll(x, 1, 1) + pltpu.roll(x, 127, 1) - 2.0 * x
-        new = x + coefs[0:1] * chain
-        for d, stride in ((1, 16), (2, 4), (3, 1)):
-            digit = lax.shift_right_logical(r64, {16: 4, 4: 2, 1: 0}[stride]) & 3
-            up = jnp.where(digit == 0, 0.0, pltpu.roll(x, stride, 0))
-            down = jnp.where(digit == 3, 0.0, pltpu.roll(x, 64 - stride, 0))
-            new = new + coefs[d : d + 1] * (up + down - 2.0 * x)
-        x = jnp.where(lane < 8, new, 0.0)
-    tiles_out[...] = pltpu.roll(x, 126, 1)[:, 0:width]
-
+    x = jnp.concatenate([summed, pltpu.roll(summed, 64, 1)], axis=0)
+    x = smooth(smooth(jnp.where(lane < 64, x, 0.0)))
+    tiles_out[...] = x[2 : 2 + width, 0:64]
+
+    for store in stores:
+        store.wait()
     for copy in rim_copies[0] + rim_copies[1] + rim2_copies + coef_copies + a_copies + b_copies:
         copy.wait_send()
 
@@ -339,14 +356,18 @@
         width = smoothing.shape[1]
         dma = pltpu.SemaphoreType.DMA
         vmem = pl.BlockSpec(memory_space=pltpu.VMEM)
-        return pl.pallas_call(
+        hbm = pl.BlockSpec(memory_space=pl.ANY)
+        line = (3 * NODES, 1, fwd.shape[-1])
+        args = (args[0].reshape(line), args[1].reshape(line), args[2], args[3].T, args[4],
+                args[5].reshape(6, 1, fwd.shape[-1]), *args[6:])
+        final, tiles = pl.pallas_call(
             functools.partial(kernel, m_size, e_size),
             out_shape=(
-                jax.ShapeDtypeStruct(fwd.shape, f32),
-                jax.ShapeDtypeStruct((64, width), f32),
+                jax.ShapeDtypeStruct(line, f32),
+                jax.ShapeDtypeStruct((width, 64), f32),
             ),
-            in_specs=[vmem] * len(args),
-            out_specs=(vmem, vmem),
+            in_specs=[hbm] * 2 + [vmem] * (len(args) - 2),
+            out_specs=(hbm, vmem),
             scratch_shapes=[
                 pltpu.VMEM((6, 144, 128), f32),
                 pltpu.VMEM((6, ROWS, 128), f32),
@@ -365,11 +386,12 @@
                 pltpu.VMEM((m_size - 1, e_size, width, 128), f32),
                 pltpu.VMEM((128, 128), f32),
                 pltpu.VMEM((e_size - 1, width, 128), f32),
-                dma((2, 2)), dma((2, 2)), dma((2,)), dma((2,)), dma((2,)), dma((2,)),
+                dma((6,)), dma((3,)), dma((2, 2)), dma((2, 2)), dma((2,)), dma((2,)), dma((2,)), dma((2,)),
                 dma((m_size - 1,)), dma((m_size - 1,)), dma((e_size - 1,)), dma((e_size - 1,)),
             ],
             compiler_params=pltpu.CompilerParams(collective_id=0, has_side_effects=True),
         )(*args)
+        return final.reshape(fwd.shape), tiles.T
 
     return jax.shard_map(
         per_device, mesh=mesh, in_specs=in_specs, out_specs=out_specs, check_vma=False

time: 33 us -> 27.2 us (0.82)
  local copies, waits for them, and re-layouts: 7.58 us -> 2.2 us
  Pallas kernels: 23.9 us -> 23.4 us
    unnamed x8 -> x4, local copies, waits for them, and re-layouts: 5.12 us -> 2.2 us
    pallas_call x2 -> x0, local copies, waits for them, and re-layouts: 2.46 us -> none  [per_device(): pl.pallas_call(functools.partial(kernel, m_size, e_size), out_shape=(jax....]
    pallas_call x1, Pallas kernels: 23.9 us -> 23.4 us  [per_device(): pl.pallas_call(functools.partial(kernel, m_size, e_size), out_shape=(jax....]
where the time goes in v2:
time: 27.2 us; the launch traced here: 26.9 us
  Pallas kernels  23.4 us (86%)
  local copies, waits for them, and re-layouts  2.2 us (8%)
  between operations  1.3 us (5%)
    pallas_call x1, Pallas kernels, per_device(): pl.pallas_call(functools.partial(kernel, m_size, e_size), out_shape=(jax....  23.4 us
    unnamed x4, local copies, waits for them, and re-layouts  2.2 us

profile of v2, /device:TPU:0, one launch (start us, length us, event | category | flops | bytes accessed | tf_op | source)
XLA Modules:
  0.0 26.9 jit_solution(10761402370104884770)
XLA Ops:
  1.3 23.4 %shard_map.104 = (f32[375,1,128]{2,1,0:T(1,128)}, f32[4,64]{1,0:T(4,128)}) custom-call(f32[375,1,128]{2,1,0:T(1,128)} %bitcast.6, f32[375,1,128]{2,1,0:T(1,128)} %bitcast.7, f32[125,125]{1,0:T(8,128)} %stiff_in.1, f32[64,125]{1,0:T(8,128)} %bitcast.9, f32[1,128]{1,0:T(1,128)} %mat_in.1, s32[6,1,128]{2,1,0:T(1,128)} %bitcast.10, s32[1,128]{1,0:T(1,128)} %dest_in.1, ...), custom_call_target="tpu_custom_call" | custom-call | tf_op jit(solution)/shard_map/pallas_call | solution.py:363
  24.7 0.0 copy-start
  24.7 1.6 %copy.14 = f32[1,3,125,128]{3,0,2,1:T(1,128)} copy(f32[1,3,125,128]{3,0,2,1:T(1,128)} %bitcast.8) | data formatting | bytes 384000
  26.4 0.0 copy-done
  26.4 0.6 %copy.15 = f32[64,4]{0,1:T(4,128)} copy(f32[64,4]{0,1:T(4,128)S(1)} %bitcast.11) | data formatting | bytes 2048
Async XLA Ops:
  24.7 1.6 %copy-start = (f32[4,64]{1,0:T(4,128)S(1)}, f32[4,64]{1,0:T(4,128)}, u32[]{:S(2)}) copy-start(f32[4,64]{1,0:T(4,128)} %get-tuple-element.5) | copy-start | bytes 3076

commit v3 on v2

--- a/solution.py
+++ b/solution.py
@@ -47,10 +47,11 @@
 
 def kernel(
     m_size, e_size,
-    fwd_in, adj_in, stiff_in, proj_in, mat_in, nb_in, dest_in, count_in, smooth_in,
+    fwd_in, adj_in, stiff_hbm, proj_hbm, mat_hbm, nb_hbm, dest_hbm, count_hbm, smooth_hbm,
     fwd_out, tiles_out,
+    stiff_in, proj_in, mat_in, nb_in, dest_in, count_in, smooth_in,
     F, N, K, S, W, IDX, LIVE, send, rim, rim2, coef, coef_in, msg, part, got, mine, got2,
-    in_s, out_s, rim_s, rim_r, rim2_s, rim2_r, coef_s, coef_r, a_s, a_r, b_s, b_r,
+    in_s, small_s, out_s, rim_s, rim_r, rim2_s, rim2_r, coef_s, coef_r, a_s, a_r, b_s, b_r, rounds,
 ):
     me = lax.axis_index("mesh")
     ev = lax.axis_index("event")
@@ -58,9 +59,32 @@
     lin = ev * m_size + me
     after = lax.rem(me + 1, m_size)
     before = lax.rem(me + m_size - 1, m_size)
-    nxt = lax.rem(lin + 1, total)
-    prv = lax.rem(lin + total - 1, total)
-    lin_id = lambda d: (lax.div(d, m_size), lax.rem(d, m_size))
+
+    barrier = pltpu.get_barrier_semaphore()
+    core = lax.rem(ev, 2)
+    chip = lax.div(ev, 2)
+    chips = e_size // 2
+    near = [((2 * chip + 1 - core, me), None)]
+    for step in (1, -1):
+        inside = (chip + step >= 0) & (chip + step < chips)
+        near += [((2 * (chip + step) + c, me), inside) for c in range(2)]
+    near_count = 1 + 2 * ((chip > 0).astype(jnp.int32) + (chip < chips - 1).astype(jnp.int32))
+
+    def greet(sem):
+        for device, inside in near:
+            if inside is None:
+                pl.semaphore_signal(sem, inc=1, device_id=device, device_id_type=MESH)
+            else:
+
+                @pl.when(inside)
+                def _():
+                    pl.semaphore_signal(sem, inc=1, device_id=device, device_id_type=MESH)
+
+    for o in range(1, m_size):
+        pl.semaphore_signal(
+            barrier, inc=1, device_id=(ev, lax.rem(me + o, m_size)), device_id_type=MESH
+        )
+    greet(barrier)
 
     loads = []
     for fc in range(6):
@@ -71,16 +95,16 @@
         load.start()
         loads.append(load)
 
-    barrier = pltpu.get_barrier_semaphore()
-    partners = [(ev, lax.rem(me + j, m_size)) for j in range(1, m_size)]
-    partners += [(lax.rem(ev + j, e_size), me) for j in range(1, e_size)]
-    partners += [lin_id(nxt), lin_id(prv)]
-    for device in partners:
-        pl.semaphore_signal(barrier, inc=1, device_id=device, device_id_type=MESH)
+    small = []
+    for n, (src, dst) in enumerate((
+        (smooth_hbm, smooth_in), (stiff_hbm, stiff_in), (nb_hbm, nb_in), (count_hbm, count_in),
+        (mat_hbm, mat_in), (proj_hbm, proj_in), (dest_hbm, dest_in),
+    )):
+        load = pltpu.make_async_copy(src, dst, small_s.at[n])
+        load.start()
+        small.append(load)
 
     lane = lax.broadcasted_iota(jnp.int32, (1, 128), 1)
-    live = jnp.where(lane < count_in[0:1, 0:1], 1.0, 0.0).astype(f32)
-    LIVE[...] = jnp.broadcast_to(live, (8, 128))
     zero8 = jnp.zeros((PAD, 128), f32)
     for fc in range(6):
         F[fc, 0:PAD, :] = zero8
@@ -101,9 +125,10 @@
             load.wait()
         send[f] = pack(3 * f)
     coef[...] = jnp.zeros((8, 128), f32)
+    small[0].wait()
     coef[0:4, 0:4] = smooth_in[...]
 
-    pl.semaphore_wait(barrier, len(partners))
+    pl.semaphore_wait(barrier, near_count + (m_size - 1))
 
     def remote(src, dst, s, r, device):
         copy = pltpu.make_async_remote_copy(
@@ -120,10 +145,16 @@
         for f in range(2)
     ]
     coef_copies = [
-        remote(coef, coef_in.at[0], coef_s.at[0], coef_r.at[0], lin_id(nxt)),
-        remote(coef, coef_in.at[1], coef_s.at[1], coef_r.at[1], lin_id(prv)),
-    ]
-
+        remote(coef, coef_in.at[0], coef_s.at[0], coef_r.at[0], (ev, after)),
+        remote(coef, coef_in.at[1], coef_s.at[1], coef_r.at[1], (ev, before)),
+    ]
+    if chips > 2:
+        greet(rounds.at[0])
+
+    for load in small[1:]:
+        load.wait()
+    live = jnp.where(lane < count_in[0:1, 0:1], 1.0, 0.0).astype(f32)
+    LIVE[...] = jnp.broadcast_to(live, (8, 128))
     for fc in range(6):
         F[fc, PAD : PAD + NODES, :] = F[fc, PAD : PAD + NODES, :] * live
 
@@ -212,7 +243,14 @@
         N[3 + c] = F[3 + c, PAD : PAD + ROWS, :] - time_square * material * st_a[c]
     K[...] = energy
     own_pass(0)
-    own_pass(3)
+    for n in range(chips - 2):
+        pl.semaphore_wait(rounds.at[n], near_count)
+        if n + 1 < chips - 2:
+            greet(rounds.at[n + 1])
+        if n == 0:
+            own_pass(3)
+    if chips <= 2:
+        own_pass(3)
 
     def keep(base):
         def store(c, t, value):
@@ -230,16 +268,12 @@
         rim_pass(3 * f, rim.at[f], keep(3 * f))
         if f == 0:
             send[2] = pack(0)
-            rim2_copies = [
-                remote(send.at[2], rim2.at[0, pl.ds(PAD, 96)], rim2_s.at[0], rim2_r.at[0], (ev, after)),
-                remote(send.at[2], rim2.at[1, pl.ds(PAD, 96)], rim2_s.at[1], rim2_r.at[1], (ev, before)),
-            ]
 
     st_a = strain(3)
     energy = K[...]
     for c in range(3):
         energy = energy + F[c, PAD : PAD + ROWS, :] * st_a[c]
-    elements = fwd_in.shape[-1]
+    elements = F.shape[-1]
     width = smooth_in.shape[1]
     scale = math.sqrt(width / elements) / STEPS
     twin = jnp.concatenate([proj_in[...], proj_in[...]], axis=0)
@@ -267,11 +301,24 @@
         for o in range(1, m_size)
     ]
 
+    rim2_copies = [
+        remote(send.at[2], rim2.at[0, pl.ds(PAD, 96)], rim2_s.at[0], rim2_r.at[0], (ev, after)),
+        remote(send.at[2], rim2.at[1, pl.ds(PAD, 96)], rim2_s.at[1], rim2_r.at[1], (ev, before)),
+    ]
+
     st_f = strain(0)
     for c in range(3):
         N[c] = N[c] - time_square * material * st_f[c]
     own_pass(0)
 
+    for copy in coef_copies:
+        copy.wait_recv()
+    coef_copies += [
+        remote(coef_in.at[0], coef_in.at[2], coef_s.at[2], coef_r.at[2],
+               (lax.rem(ev + 1, e_size), me)),
+        remote(coef_in.at[1], coef_in.at[3], coef_s.at[3], coef_r.at[3],
+               (lax.rem(ev + e_size - 1, e_size), me)),
+    ]
     for copy in a_copies:
         copy.wait_recv()
     mine_sum = msg[me]
@@ -300,11 +347,13 @@
         store.start()
         stores.append(store)
 
-    for copy in coef_copies:
+    for copy in coef_copies[2:]:
         copy.wait_recv()
     own_coef = pltpu.roll(coef[...], 2, 1)
-    left = jnp.where(lin > 0, coef_in[0], 0.0)
-    right = jnp.where(lin < total - 1, coef_in[1], 0.0)
+    left = jnp.where(lin > 0, jnp.where(me > 0, coef_in[0], coef_in[2]), 0.0)
+    right = jnp.where(
+        lin < total - 1, jnp.where(me < m_size - 1, coef_in[1], coef_in[3]), 0.0
+    )
     left = jnp.where(lane < 2, pltpu.roll(left, 126, 1), 0.0)
     right = pltpu.roll(right, 6, 1)
     mine[...] = jnp.zeros((128, 128), f32)
@@ -356,19 +405,20 @@
         width = smoothing.shape[1]
         dma = pltpu.SemaphoreType.DMA
         vmem = pl.BlockSpec(memory_space=pltpu.VMEM)
-        hbm = pl.BlockSpec(memory_space=pl.ANY)
+        hbm = pl.BlockSpec(memory_space=pltpu.HBM)
         line = (3 * NODES, 1, fwd.shape[-1])
         args = (args[0].reshape(line), args[1].reshape(line), args[2], args[3].T, args[4],
                 args[5].reshape(6, 1, fwd.shape[-1]), *args[6:])
         final, tiles = pl.pallas_call(
             functools.partial(kernel, m_size, e_size),
             out_shape=(
-                jax.ShapeDtypeStruct(line, f32),
-                jax.ShapeDtypeStruct((width, 64), f32),
+                pltpu.VMEM(line, f32),
+                pltpu.VMEM((width, 64), f32),
             ),
-            in_specs=[hbm] * 2 + [vmem] * (len(args) - 2),
-            out_specs=(hbm, vmem),
-            scratch_shapes=[
+            in_specs=[hbm] * len(args),
+            out_specs=(vmem, vmem),
+            scratch_shapes=[pltpu.VMEM(x.shape, x.dtype) for x in args[2:]]
+            + [
                 pltpu.VMEM((6, 144, 128), f32),
                 pltpu.VMEM((6, ROWS, 128), f32),
                 pltpu.VMEM((ROWS, 128), f32),
@@ -380,14 +430,15 @@
                 pltpu.VMEM((2, 2, 144, 128), f32),
                 pltpu.VMEM((2, 144, 128), f32),
                 pltpu.VMEM((8, 128), f32),
-                pltpu.VMEM((2, 8, 128), f32),
+                pltpu.VMEM((4, 8, 128), f32),
                 pltpu.VMEM((m_size, e_size, width, 128), f32),
                 pltpu.VMEM((e_size, width, 128), f32),
                 pltpu.VMEM((m_size - 1, e_size, width, 128), f32),
                 pltpu.VMEM((128, 128), f32),
                 pltpu.VMEM((e_size - 1, width, 128), f32),
-                dma((6,)), dma((3,)), dma((2, 2)), dma((2, 2)), dma((2,)), dma((2,)), dma((2,)), dma((2,)),
+                dma((6,)), dma((7,)), dma((3,)), dma((2, 2)), dma((2, 2)), dma((2,)), dma((2,)), dma((4,)), dma((4,)),
                 dma((m_size - 1,)), dma((m_size - 1,)), dma((e_size - 1,)), dma((e_size - 1,)),
+                pltpu.SemaphoreType.REGULAR((max(e_size // 2 - 2, 1),)),
             ],
             compiler_params=pltpu.CompilerParams(collective_id=0, has_side_effects=True),
         )(*args)

time: 27.2 us -> 24 us (0.88)
  Pallas kernels: 23.4 us -> 21.3 us
  local copies, waits for them, and re-layouts: 2.2 us -> 1.26 us
    pallas_call x1, Pallas kernels: 23.4 us -> 21.3 us  [per_device(): pl.pallas_call(functools.partial(kernel, m_size, e_size), out_shape=(pltp...]
    unnamed x4 -> x2, local copies, waits for them, and re-layouts: 2.2 us -> 1.26 us
where the time goes in v3:
time: 24 us; the launch traced here: 23.8 us
  Pallas kernels  21.3 us (89%)
  between operations  1.29 us (5%)
  local copies, waits for them, and re-layouts  1.26 us (5%)
    pallas_call x1, Pallas kernels, per_device(): pl.pallas_call(functools.partial(kernel, m_size, e_size), out_shape=(pltp...  21.3 us
    unnamed x2, local copies, waits for them, and re-layouts  1.26 us

profile of v3, /device:TPU:0, one launch (start us, length us, event | category | flops | bytes accessed | tf_op | source)
XLA Modules:
  0.0 23.8 jit_solution(1407819713899728079)
XLA Ops:
  1.3 21.3 %shard_map.104 = (f32[375,1,128]{2,1,0:T(1,128)S(1)}, f32[4,64]{1,0:T(4,128)S(1)}) custom-call(f32[375,1,128]{2,1,0:T(1,128)} %bitcast.8, f32[375,1,128]{2,1,0:T(1,128)} %bitcast.9, f32[125,125]{1,0:T(8,128)} %stiff_hbm.1, f32[64,125]{1,0:T(8,128)} %bitcast.10, f32[1,128]{1,0:T(1,128)} %mat_hbm.1, s32[6,1,128]{2,1,0:T(1,128)} %bitcast.11, ...), custom_call_target="tpu_custom_call" | custom-call | tf_op jit(solution)/shard_map/pallas_call | solution.py:412
  22.6 0.7 %copy.13 = f32[1,3,125,128]{3,0,2,1:T(1,128)} copy(f32[1,3,125,128]{3,0,2,1:T(1,128)S(1)} %bitcast.6) | data formatting | bytes 384000
  23.2 0.6 %copy.14 = f32[64,4]{0,1:T(4,128)} copy(f32[64,4]{0,1:T(4,128)S(1)} %bitcast.7) | data formatting | bytes 2048

commit v4 on v3

--- a/solution.py
+++ b/solution.py
@@ -137,12 +137,22 @@
         copy.start()
         return copy
 
+    paired = m_size == 4
+    first = 1 - lax.rem(me, 2) if paired else 0
+    second = 1 - first
+    rows = pl.ds(PAD, 96)
+
+    def to_sides(src, land, sends, recvs):
+        slots = (second, first) if paired else (first, second)
+        return [
+            remote(src, land.at[slot, rows], sends.at[n], recvs.at[n],
+                   (ev, jnp.where(slot == 0, after, before)))
+            for n, slot in enumerate(slots)
+        ]
+
     rim_copies = [
-        [
-            remote(send.at[f], rim.at[f, 0, pl.ds(PAD, 96)], rim_s.at[f, 0], rim_r.at[f, 0], (ev, after)),
-            remote(send.at[f], rim.at[f, 1, pl.ds(PAD, 96)], rim_s.at[f, 1], rim_r.at[f, 1], (ev, before)),
-        ]
-        for f in range(2)
+        to_sides(send.at[0], rim.at[0], rim_s.at[0], rim_r.at[0]),
+        to_sides(send.at[1], rim.at[1], rim_s.at[1], rim_r.at[1]),
     ]
     coef_copies = [
         remote(coef, coef_in.at[0], coef_s.at[0], coef_r.at[0], (ev, after)),
@@ -187,19 +197,26 @@
         both = mm(s_hi, hi) + (mm(s_hi, lo) + mm(s_lo, hi))
         return [both[:, 128 * c : 128 * (c + 1)] for c in range(3)]
 
+    def face_sums(read, offset, relative_to):
+        sums = [None] * (ROWS // 8)
+        for f in range(6):
+            at = IDX[f] if offset is None else (IDX[f] & 31) + offset
+            here = IDX[6 + f] == relative_to
+            for t in range(ROWS // 8):
+                if f in TILE_FACES[t]:
+                    g = jnp.where(here, pick(read(8 * t + PAD + SHIFT[f]), at), 0.0)
+                    g = g * W[f, 8 * t : 8 * t + 8, :]
+                    sums[t] = g if sums[t] is None else sums[t] + g
+        return sums
+
     def own_pass(base):
         def body(c, carry):
+            sums = face_sums(lambda low: F[base + c, low : low + 8, :], None, 0)
             for t in range(ROWS // 8):
-                acc = jnp.zeros((8, 128), f32)
-                for f in TILE_FACES[t]:
-                    x = F[base + c, 8 * t + PAD + SHIFT[f] : 8 * t + 2 * PAD + SHIFT[f], :]
-                    g = pick(x, IDX[f])
-                    acc = acc + jnp.where(IDX[6 + f] == 0, g, 0.0) * W[f, 8 * t : 8 * t + 8, :]
+                at = pl.ds(8 * t, 8)
                 v = F[base + c, 8 * t + PAD : 8 * t + 2 * PAD, :]
-                acc = acc - W[6, 8 * t : 8 * t + 8, :] * v
-                N[base + c, 8 * t : 8 * t + 8, :] = (
-                    N[base + c, 8 * t : 8 * t + 8, :] + (time_square * penalty) * acc
-                )
+                acc = sums[t] - W[6, at, :] * v
+                N[base + c, at, :] = N[base + c, at, :] + (time_square * penalty) * acc
             return carry
 
         lax.fori_loop(0, 3, body, 0)
@@ -214,24 +231,23 @@
         ref[0:PAD, :] = zero8
         ref[PAD + 128 : PAD + 136, :] = zero8
 
-    def rim_pass(base, ref, store):
+    def rim_pass(base, ref, side, store):
+        relative_to = jnp.where(side == 1, 1, m_size - 1)
+
         def body(c, carry):
-            live8 = LIVE[...]
+            sums = face_sums(lambda low: ref[low : low + 8, :], 32 * c, relative_to)
             for t in range(ROWS // 8):
-                acc = jnp.zeros((8, 128), f32)
-                for f in TILE_FACES[t]:
-                    low = 8 * t + PAD + SHIFT[f]
-                    at = (IDX[f] & 31) + 32 * c
-                    r = IDX[6 + f]
-                    g = jnp.where(
-                        r == 1, pick(ref[1, low : low + 8, :], at), pick(ref[0, low : low + 8, :], at)
-                    )
-                    acc = acc + jnp.where(r == 0, 0.0, g) * W[f, 8 * t : 8 * t + 8, :]
                 old = N[base + c, 8 * t : 8 * t + 8, :]
-                store(c, t, live8 * (old + (time_square * penalty) * acc))
+                store(c, t, old + (time_square * penalty) * sums[t])
             return carry
 
         lax.fori_loop(0, 3, body, 0)
+
+    def add(base):
+        def store(c, t, value):
+            N[base + c, 8 * t : 8 * t + 8, :] = value
+
+        return store
 
     st_f = strain(0)
     st_a = strain(3)
@@ -254,6 +270,7 @@
 
     def keep(base):
         def store(c, t, value):
+            value = LIVE[...] * value
             at = pl.ds(8 * t + PAD, 8)
             if base == 0:
                 N[c, 8 * t : 8 * t + 8, :] = 2.0 * value - F[c, at, :]
@@ -262,10 +279,15 @@
         return store
 
     for f in range(2):
-        for side in range(2):
-            rim_copies[f][side].wait_recv()
-            unpack(rim.at[f, side])
-        rim_pass(3 * f, rim.at[f], keep(3 * f))
+        rim_copies[f][0].wait_recv()
+        near_ref = rim.at[f, first]
+        unpack(near_ref)
+        rim_pass(3 * f, near_ref, first, add(3 * f))
+    for f in range(2):
+        rim_copies[f][1].wait_recv()
+        far_ref = rim.at[f, second]
+        unpack(far_ref)
+        rim_pass(3 * f, far_ref, second, keep(3 * f))
         if f == 0:
             send[2] = pack(0)
 
@@ -282,8 +304,7 @@
     k_hi, k_lo = split(K[0:NODES, :])
     blocks = (mm(t_hi, k_hi) + (mm(t_hi, k_lo) + mm(t_lo, k_hi))) * scale
     b_hi, b_lo = split(blocks)
-    rows = total * width
-    row = lax.broadcasted_iota(jnp.int32, (rows, 128), 0)
+    row = lax.broadcasted_iota(jnp.int32, (total * width, 128), 0)
     owner = lax.div(row, width)
     tile = width * (lax.rem(owner, e_size) * m_size + lax.div(owner, e_size)) + lax.rem(row, width)
     dest = dest_in[...]
@@ -301,10 +322,7 @@
         for o in range(1, m_size)
     ]
 
-    rim2_copies = [
-        remote(send.at[2], rim2.at[0, pl.ds(PAD, 96)], rim2_s.at[0], rim2_r.at[0], (ev, after)),
-        remote(send.at[2], rim2.at[1, pl.ds(PAD, 96)], rim2_s.at[1], rim2_r.at[1], (ev, before)),
-    ]
+    rim2_copies = to_sides(send.at[2], rim2, rim2_s, rim2_r)
 
     st_f = strain(0)
     for c in range(3):
@@ -331,14 +349,14 @@
         for o in range(1, e_size)
     ]
 
-    for side in range(2):
-        rim2_copies[side].wait_recv()
-        unpack(rim2.at[side])
-
     def final(c, t, value):
-        N[c, 8 * t : 8 * t + 8, :] = value
-
-    rim_pass(0, rim2, final)
+        N[c, 8 * t : 8 * t + 8, :] = LIVE[...] * value
+
+    for n, side in enumerate((first, second)):
+        rim2_copies[n].wait_recv()
+        ref = rim2.at[side]
+        unpack(ref)
+        rim_pass(0, ref, side, add(0) if n == 0 else final)
     stores = []
     for c in range(3):
         store = pltpu.make_async_copy(

time: 24 us -> 23.2 us (0.967)
  Pallas kernels: 21.3 us -> 20.5 us
    pallas_call x1, Pallas kernels: 21.3 us -> 20.5 us  [per_device(): pl.pallas_call(functools.partial(kernel, m_size, e_size), out_shape=(pltp...]
where the time goes in v4:
time: 23.2 us; the launch traced here: 23 us
  Pallas kernels  20.5 us (88%)
  between operations  1.29 us (6%)
  local copies, waits for them, and re-layouts  1.26 us (5%)
    pallas_call x1, Pallas kernels, per_device(): pl.pallas_call(functools.partial(kernel, m_size, e_size), out_shape=(pltp...  20.5 us
    unnamed x2, local copies, waits for them, and re-layouts  1.26 us

profile of v4, /device:TPU:0, one launch (start us, length us, event | category | flops | bytes accessed | tf_op | source)
XLA Modules:
  0.0 23.0 jit_solution(9462650505118679963)
XLA Ops:
  1.3 20.5 %shard_map.104 = (f32[375,1,128]{2,1,0:T(1,128)S(1)}, f32[4,64]{1,0:T(4,128)S(1)}) custom-call(f32[375,1,128]{2,1,0:T(1,128)} %bitcast.8, f32[375,1,128]{2,1,0:T(1,128)} %bitcast.9, f32[125,125]{1,0:T(8,128)} %stiff_hbm.1, f32[64,125]{1,0:T(8,128)} %bitcast.10, f32[1,128]{1,0:T(1,128)} %mat_hbm.1, s32[6,1,128]{2,1,0:T(1,128)} %bitcast.11, ...), custom_call_target="tpu_custom_call" | custom-call | tf_op jit(solution)/shard_map/pallas_call | solution.py:430
  21.8 0.7 %copy.13 = f32[1,3,125,128]{3,0,2,1:T(1,128)} copy(f32[1,3,125,128]{3,0,2,1:T(1,128)S(1)} %bitcast.6) | data formatting | bytes 384000
  22.4 0.6 %copy.14 = f32[64,4]{0,1:T(4,128)} copy(f32[64,4]{0,1:T(4,128)S(1)} %bitcast.7) | data formatting | bytes 2048
